TPU v7x, 32 devices: a whole 2x2x4 slice. The times are simulated.
32 devices in a mesh: vblk: 8 (over y, x, core), pair: 4 (over z).
Axes of the slice: x: 2, y: 2, z: 4, core: 2. Of those that a mesh axis runs over, the one named last changes fastest.
Arguments:
- amplitudes: bfloat16 [128, 384, 384], P(('vblk', 'pair')), may hold values from -6 to 6
- domain_mask: int32 [128, 3], P(('vblk', 'pair')), may hold values from 0 to 1, as said below
- centers: int32 [128], P(('vblk', 'pair')), may hold values from 0 to 7, as said below
- chol_panel: bfloat16 [8, 8, 5, 128, 128], P('vblk', None, None, 'pair'), may hold values from -0.3125 to 0.3125
Outputs:
- residual_tiles: float32 [128, 384, 384], P(('vblk', 'pair'))
Inputs may be any that keep to these rules, and one draw needn't show every extreme that they name: centers[p] differs from p // 16 (the block of the region that holds pair p) by at most 1, and by exactly 1 in both directions for some pairs. `domain_mask`: the middle column of the window (column 1 for a window of 3 blocks) is 1 for every pair; column k is 0 where the window block centers + k minus the middle index lies outside 0 to 7.
All inputs are finite; a program needn't handle non-finite values.
Results may differ from a plain program's by a relative error of at most 0.0029.
Values may be sent and summed in bfloat16 or wider, within the bound.
No kernel may reach another device: no remote copies, remote signals or barrier semaphores. Data moves between devices by JAX's collectives and lax.ppermute only.
A program may use at most 128 MiB of HBM per device.

v0:
```python
import jax
import jax.numpy as jnp
from jax import lax
from jax.sharding import PartitionSpec as P

VB = 128
DW = 3
RCH = 1


def from_behind(value, axis, steps):
    count = lax.axis_size(axis)
    first, last = (max(0, -steps), min(count, count - steps))
    return lax.ppermute(value, axis, [(source, source + steps) for source in range(first, last)])


def assemble(window):
    strips = []
    for a in range(DW):
        strips.append(
            jnp.concatenate([window[..., a, :, b - a + DW - 1, :, :] for b in range(DW)], axis=-1)
        )
    return jnp.concatenate(strips, axis=-2)


def local(amplitudes, domain_mask, centers, chol_panel):
    halfwidth = (DW - 1) // 2
    furthest = RCH + halfwidth
    whole = lax.all_gather(chol_panel, "pair", axis=3, tiled=True)
    nearby = []
    for distance in range(-furthest, furthest + 1):
        if distance == 0:
            nearby.append(whole)
        else:
            nearby.append(from_behind(whole, "vblk", -distance))
    neighbourhood = jnp.concatenate(nearby, axis=0)
    position = lax.axis_index("vblk")
    offset = centers - position + furthest - halfwidth
    row_index = offset[:, None] + jnp.arange(DW, dtype=jnp.int32)[None, :]
    window = jnp.take(neighbourhood, row_index, axis=0)
    blocks = assemble(window)
    live_cols = jnp.repeat(domain_mask, VB, axis=1) > 0
    keep_tile = live_cols[:, :, None] & live_cols[:, None, :]
    masked = jnp.where(keep_tile, amplitudes, jnp.zeros_like(amplitudes))
    half_product = jnp.einsum(
        "pqij,pjk->pqik", blocks, masked, preferred_element_type=jnp.float32
    ).astype(jnp.bfloat16)
    ladder = jnp.einsum("pqik,pqlk->pil", half_product, blocks, preferred_element_type=jnp.float32)
    return jnp.where(keep_tile, ladder, jnp.zeros_like(ladder))


def solution(mesh):
    return jax.shard_map(
        local,
        mesh=mesh,
        in_specs=(
            P(("vblk", "pair"), None, None),
            P(("vblk", "pair"), None),
            P(("vblk", "pair")),
            P("vblk", None, None, "pair", None),
        ),
        out_specs=P(("vblk", "pair"), None, None),
        check_vma=False,
    )
```

profile of v0, /device:TPU:0, one launch (start us, length us, event | category | flops | bytes accessed | tf_op | source)
XLA Modules:
  0.0 181.5 jit_solution(7642532700543118598)
XLA Ops:
  6.5 0.0 all-gather.2.cloned.1.call-start
  6.5 0.7 all-gather.2.cloned.1.call-update
  7.3 37.1 %all-gather.2.cloned.1.call-done = bf16[1,8,5,128,128]{4,3,2,1,0:T(8,128)(2,1)} async-done(((bf16[1,8,5,32,128]{4,3,2,1,0:T(8,128)(2,1)}), bf16[1,8,5,128,128]{4,3,2,1,0:T(8,128)(2,1)}) %all-gather.2.cloned.1.call-update) | async-done | bytes 1310736 | tf_op jit(solution)/shard_map/all_gather | solution.py:29
  44.4 3.4 %collective-permute-start = (bf16[1,8,5,128,128]{4,3,2,1,0:T(8,128)(2,1)}, bf16[1,8,5,128,128]{4,3,2,1,0:T(8,128)(2,1)S(1)}, u32[]{:S(2)}, u32[]{:S(2)}) collective-permute-start(bf16[1,8,5,128,128]{4,3,2,1,0:T(8,128)(2,1)} %all-gather.2.cloned.1.call-done), channel_id=1, source_target_pairs={{0,8},{4,12},{8,16},{12,20},{16,24},{20,28},{1,9},{5,13},{9,17},{1... | collective-permute-start | bytes 3932168 | tf_op jit(solution)/shard_map/ppermute | solution.py:14
  47.8 2.4 %collective-permute-start.1 = (bf16[1,8,5,128,128]{4,3,2,1,0:T(8,128)(2,1)}, bf16[1,8,5,128,128]{4,3,2,1,0:T(8,128)(2,1)}, u32[]{:S(2)}, u32[]{:S(2)}) collective-permute-start(bf16[1,8,5,128,128]{4,3,2,1,0:T(8,128)(2,1)} %all-gather.2.cloned.1.call-done), channel_id=1, source_target_pairs={{0,4},{4,8},{8,12},{12,16},{16,20},{20,24},{24,28},{1,5},{5,9},{9,... | collective-permute-start | bytes 3932168 | tf_op jit(solution)/shard_map/ppermute | solution.py:14
  50.2 0.7 subtract_add_fusion
  50.8 1.3 collective-permute-start.2
  52.1 0.1 compare_select_fusion
  52.2 0.1 reshape.71
  52.3 1.3 collective-permute-start.3
  53.6 0.1 fusion.17
  53.6 0.1 copy.7
  53.8 0.7 broadcast_compare_fusion
  54.4 0.1 copy.6
  54.6 0.1 broadcast_bitcast_fusion
  54.6 22.6 %collective-permute-done = bf16[1,8,5,128,128]{4,3,2,1,0:T(8,128)(2,1)S(1)} collective-permute-done((bf16[1,8,5,128,128]{4,3,2,1,0:T(8,128)(2,1)}, bf16[1,8,5,128,128]{4,3,2,1,0:T(8,128)(2,1)S(1)}, u32[]{:S(2)}, u32[]{:S(2)}) %collective-permute-start) | collective-permute-done | bytes 1310752 | tf_op jit(solution)/shard_map/ppermute | solution.py:14
  77.3 1.2 constant_dynamic-update-slice_fusion.4
  78.4 0.0 collective-permute-done.1
  78.4 2.5 %constant_dynamic-update-slice_fusion.3 = bf16[5,8,5,128,128]{4,3,2,1,0:T(8,128)(2,1)} fusion(bf16[5,8,5,128,128]{4,3,2,1,0:T(8,128)(2,1)} %constant_dynamic-update-slice_fusion.4, bf16[1,8,5,128,128]{4,3,2,1,0:T(8,128)(2,1)} %collective-permute-done.1), kind=kLoop, calls=%fused_computation.24 | loop fusion | bytes 2621440
  81.0 2.5 %constant_dynamic-update-slice_fusion.2 = bf16[5,8,5,128,128]{4,3,2,1,0:T(8,128)(2,1)} fusion(bf16[5,8,5,128,128]{4,3,2,1,0:T(8,128)(2,1)} %constant_dynamic-update-slice_fusion.3, bf16[1,8,5,128,128]{4,3,2,1,0:T(8,128)(2,1)} %all-gather.2.cloned.1.call-done), kind=kLoop, calls=%fused_computation.23 | loop fusion | bytes 2621440
  83.5 0.0 collective-permute-done.2
  83.5 1.1 constant_dynamic-update-slice_fusion.1
  84.6 48.8 %collective-permute-done.3 = bf16[1,8,5,128,128]{4,3,2,1,0:T(8,128)(2,1)} collective-permute-done((bf16[1,8,5,128,128]{4,3,2,1,0:T(8,128)(2,1)}, bf16[1,8,5,128,128]{4,3,2,1,0:T(8,128)(2,1)}, u32[]{:S(2)}, u32[]{:S(2)}) %collective-permute-start.3) | collective-permute-done | bytes 1310752 | tf_op jit(solution)/shard_map/ppermute | solution.py:14
  133.5 2.6 %constant_dynamic-update-slice_fusion = bf16[5,8,5,128,128]{4,3,2,1,0:T(8,128)(2,1)} fusion(bf16[5,8,5,128,128]{4,3,2,1,0:T(8,128)(2,1)} %constant_dynamic-update-slice_fusion.1, bf16[1,8,5,128,128]{4,3,2,1,0:T(8,128)(2,1)} %collective-permute-done.3), kind=kLoop, calls=%fused_computation.21 | loop fusion | bytes 2621440 | tf_op jit(solution)/shard_map/concatenate | solution.py:36
  136.0 10.0 %gather_fusion = bf16[12,8,5,128,128]{4,3,2,1,0:T(8,128)(2,1)} fusion(bf16[5,8,5,128,128]{4,3,2,1,0:T(8,128)(2,1)} %constant_dynamic-update-slice_fusion, s32[1024]{0:T(1024)S(1)} %pad_clamp_fusion), kind=kCustom, calls=%fused_computation | custom fusion | bytes 31457328 | tf_op jit(solution)/shard_map/jit(_take)/gather | solution.py:40
  146.0 8.3 %copy_select_fusion = bf16[4,3,8,5,128,128]{5,4,2,0,3,1:T(8,128)(2,1)S(1)} fusion(bf16[4,3,8,5,128,128]{5,4,3,2,1,0:T(8,128)(2,1)} %bitcast.39, pred[4,3]{0,1:T(4,128)(4,1)S(1)} %copy.7), kind=kLoop, calls=%fused_computation.1 | loop fusion | flops 7864320 | bytes 31457292 | tf_op jit(solution)/shard_map/jit(_take)/select_n | solution.py:40
  154.3 0.0 copy-start
  154.3 3.3 %slice_bitcast_fusion.8 = (bf16[4,8,128,128]{3,2,1,0:T(8,128)(2,1)S(1)}, bf16[4,8,128,128]{3,2,1,0:T(8,128)(2,1)S(1)}, bf16[4,8,128,128]{3,2,1,0:T(8,128)(2,1)S(...) fusion(bf16[4,3,8,5,128,128]{5,4,2,0,3,1:T(8,128)(2,1)S(1)} %co, ...), kind=kLoop, calls=%fused_computation.19 | loop fusion | bytes 18874368 | tf_op jit(solution)/shard_map/squeeze | solution.py:21
  157.7 0.0 copy-done
  157.7 8.3 %fusion.29 = bf16[4,8,384,384]{3,2,1,0:T(8,128)(2,1)} fusion(bf16[4,8,128,128]{3,2,1,0:T(8,128)(2,1)S(1)} %get-tuple-element.6, bf16[4,8,128,128]{3,2,1,0:T(8,128)(2,1)S(1)} %get-tuple-element.7, bf16[4,8,128,128]{3,2,1,0:T(8,128)(2,1)S(1)} %get-tuple-element.8, bf16[4,8,128,128]{3,2,1,0:T(8,128)(2,1)S(1)} %get-tuple-element.9, ...), kind=kOutput, calls=%fused_computation.4.clone.clone.clone.2 | convolution fusion | flops 3714711552 | bytes 20055552 | tf_op jit(solution)/shard_map/pqij,pjk->pqik/dot_general | solution.py:45
  165.9 8.7 %and_select_fusion = f32[4,384,384]{2,1,0:T(8,128)} fusion(bf16[4,8,128,128]{3,2,1,0:T(8,128)(2,1)S(1)} %get-tuple-element.6, bf16[4,8,128,128]{3,2,1,0:T(8,128)(2,1)S(1)} %get-tuple-element.7, bf16[4,8,128,128]{3,2,1,0:T(8,128)(2,1)S(1)} %get-tuple-element.8, bf16[4,8,128,128]{3,2,1,0:T(8,128)(2,1)S(1)} %get-tuple-element.9, ...), kind=kOutput, calls=%fused_computation.6 | convolution fusion | flops 3709992960 | bytes 21235200 | tf_op jit(solution)/shard_map/pqik,pqlk->pil/dot_general | solution.py:48
  (1 shorter events, 0.0 us)
Async XLA Ops:
  6.5 37.8 %all-gather.2.cloned.1.call-start = ((), (), s32[]{:S(2)}) async-start(), calls=%async_computation | async-start | bytes 1638400 | tf_op jit(solution)/shard_map/all_gather | solution.py:29
  44.4 32.9 %collective-permute-start = (bf16[1,8,5,128,128]{4,3,2,1,0:T(8,128)(2,1)}, bf16[1,8,5,128,128]{4,3,2,1,0:T(8,128)(2,1)S(1)}, u32[]{:S(2)}, u32[]{:S(2)}) collective-permute-start(bf16[1,8,5,128,128]{4,3,2,1,0:T(8,128)(2,1)} %all-gather.2.cloned.1.call-done), channel_id=1, source_target_pairs={{0,8},{4,12},{8,16},{12,20},{16,24},{20,28},{1,9},{5,13},{9,17},{1... | collective-permute-start | bytes 3932168 | tf_op jit(solution)/shard_map/ppermute | solution.py:14
  47.8 30.6 %collective-permute-start.1 = (bf16[1,8,5,128,128]{4,3,2,1,0:T(8,128)(2,1)}, bf16[1,8,5,128,128]{4,3,2,1,0:T(8,128)(2,1)}, u32[]{:S(2)}, u32[]{:S(2)}) collective-permute-start(bf16[1,8,5,128,128]{4,3,2,1,0:T(8,128)(2,1)} %all-gather.2.cloned.1.call-done), channel_id=1, source_target_pairs={{0,4},{4,8},{8,12},{12,16},{16,20},{20,24},{24,28},{1,5},{5,9},{9,... | collective-permute-start | bytes 3932168 | tf_op jit(solution)/shard_map/ppermute | solution.py:14
  50.8 32.6 %collective-permute-start.2 = (bf16[1,8,5,128,128]{4,3,2,1,0:T(8,128)(2,1)}, bf16[1,8,5,128,128]{4,3,2,1,0:T(8,128)(2,1)S(1)}, u32[]{:S(2)}, u32[]{:S(2)}) collective-permute-start(bf16[1,8,5,128,128]{4,3,2,1,0:T(8,128)(2,1)} %all-gather.2.cloned.1.call-done), channel_id=1, source_target_pairs={{4,0},{8,4},{12,8},{16,12},{20,16},{24,20},{28,24},{5,1},{9,5},{13... | collective-permute-start | bytes 3932168 | tf_op jit(solution)/shard_map/ppermute | solution.py:14
  52.3 81.2 %collective-permute-start.3 = (bf16[1,8,5,128,128]{4,3,2,1,0:T(8,128)(2,1)}, bf16[1,8,5,128,128]{4,3,2,1,0:T(8,128)(2,1)}, u32[]{:S(2)}, u32[]{:S(2)}) collective-permute-start(bf16[1,8,5,128,128]{4,3,2,1,0:T(8,128)(2,1)} %all-gather.2.cloned.1.call-done), channel_id=1, source_target_pairs={{8,0},{12,4},{16,8},{20,12},{24,16},{28,20},{9,1},{13,5},{17,9},{2... | collective-permute-start | bytes 3932168 | tf_op jit(solution)/shard_map/ppermute | solution.py:14
  154.3 3.4 %copy-start = (bf16[4,384,384]{2,1,0:T(8,128)(2,1)S(1)}, bf16[4,384,384]{2,1,0:T(8,128)(2,1)}, u32[]{:S(2)}) copy-start(bf16[4,384,384]{2,1,0:T(8,128)(2,1)} %param.4) | copy-start | bytes 3538948
Sparse Core Ops, SparseCore 0:
  8.9 35.3 all-gather.1
where the time goes:
time: 182 us
  waiting for transfers between devices  109 us (60%)
  local copies, waits for them, and re-layouts  23.7 us (13%)
  matrix products  17 us (9%)
  between operations  13.5 us (7%)
  other arithmetic  9.76 us (5%)
  starting transfers between devices  8.37 us (5%)
    ppermute x4, waiting for transfers between devices, from_behind(): lax.ppermute(value, axis, [(source, source + steps) for source in range(f...  71.4 us
    all_gather x1, waiting for transfers between devices, local(): whole = lax.all_gather(chol_panel, 'pair', axis=3, tiled=True)  37.1 us
    gather x1, local copies, waits for them, and re-layouts, local(): window = jnp.take(neighbourhood, row_index, axis=0)  10 us
    dot_general x1, matrix products, local(): jnp.einsum('pqik,pqlk->pil', half_product, blocks, preferred_element_type...  8.71 us
    ppermute x4, starting transfers between devices, from_behind(): lax.ppermute(value, axis, [(source, source + steps) for source in range(f...  8.37 us
    select_n x2, other arithmetic, local(): window = jnp.take(neighbourhood, row_index, axis=0)  8.33 us
    dot_general x1, matrix products, local(): jnp.einsum('pqij,pjk->pqik', blocks, masked, preferred_element_type=jnp.f...  8.28 us
    unnamed x6, local copies, waits for them, and re-layouts  7.38 us
  transfers between devices with their start and end apart: 5, of which 3 were waited for; matrix products, arithmetic and copies ran while one was open for 5% of the time, Pallas kernels for 0%

commit v1 on v0

--- a/solution.py
+++ b/solution.py
@@ -6,6 +6,31 @@
 VB = 128
 DW = 3
 RCH = 1
+
+
+def detail_targets_over_axis(content):
+    high = lax.axis_size("pair")
+    then = lax.axis_index("pair")
+    found_now, y1, response = (high, then, content.shape[3])
+    windows = [(k, (k + 1) % found_now) for k in range(found_now)]
+    queue = [(k, (k - 1) % found_now) for k in range(found_now)]
+    v_next = jnp.zeros(
+        (*content.shape[:3], found_now * response, *content.shape[4:]), content.dtype
+    )
+    v_next = lax.dynamic_update_slice_in_dim(v_next, content, y1 * response, axis=3)
+    y_new = y2 = content
+    lower = found_now // 2
+    for q in tuple(range(1, lower + 1)):
+        y_new = lax.ppermute(y_new, axis_name="pair", perm=windows)
+        v_next = lax.dynamic_update_slice_in_dim(
+            v_next, y_new, (y1 - q) % found_now * response, axis=3
+        )
+        if q < found_now - lower:
+            y2 = lax.ppermute(y2, axis_name="pair", perm=queue)
+            v_next = lax.dynamic_update_slice_in_dim(
+                v_next, y2, (y1 + q) % found_now * response, axis=3
+            )
+    return v_next
 
 
 def from_behind(value, axis, steps):
@@ -26,7 +51,7 @@
 def local(amplitudes, domain_mask, centers, chol_panel):
     halfwidth = (DW - 1) // 2
     furthest = RCH + halfwidth
-    whole = lax.all_gather(chol_panel, "pair", axis=3, tiled=True)
+    whole = detail_targets_over_axis(chol_panel)
     nearby = []
     for distance in range(-furthest, furthest + 1):
         if distance == 0:

time: 182 us -> 157 us (0.86)
  waiting for transfers between devices: 109 us -> 90.5 us
  between operations: 13.5 us -> 0.11 us
  starting transfers between devices: 8.37 us -> 13.5 us
    all_gather x1 -> x0, waiting for transfers between devices: 37.1 us -> none  [local(): whole = lax.all_gather(chol_panel, 'pair', axis=3, tiled=True)]
    ppermute x0 -> x3, waiting for transfers between devices: none -> 20.6 us  [the longest x2 16.1 us: detail_targets_over_axis(): y_new = lax.ppermute(y_new, axis_name='pair', perm=windows)]
    ppermute x0 -> x3, starting transfers between devices: none -> 5.05 us  [the longest x2 3.03 us: detail_targets_over_axis(): y_new = lax.ppermute(y_new, axis_name='pair', perm=windows)]
  transfers between devices with their start and end apart: 5 -> 7, of which waited for: 3 -> 5; matrix products, arithmetic and copies ran while one was open for 5% -> 7% of each run, Pallas kernels for 0% -> 0%
where the time goes in v1:
time: 157 us; the launch traced here: 156 us
  waiting for transfers between devices  90.5 us (58%)
  local copies, waits for them, and re-layouts  25.5 us (16%)
  matrix products  17 us (11%)
  starting transfers between devices  13.5 us (9%)
  other arithmetic  9.76 us (6%)
    ppermute x4, waiting for transfers between devices, from_behind(): lax.ppermute(value, axis, [(source, source + steps) for source in range(f...  69.9 us
    ppermute x2, waiting for transfers between devices, detail_targets_over_axis(): y_new = lax.ppermute(y_new, axis_name='pair', perm=windows)  16.1 us
    gather x1, local copies, waits for them, and re-layouts, local(): window = jnp.take(neighbourhood, row_index, axis=0)  10 us
    dot_general x1, matrix products, local(): jnp.einsum('pqik,pqlk->pil', half_product, blocks, preferred_element_type...  8.71 us
    ppermute x4, starting transfers between devices, from_behind(): lax.ppermute(value, axis, [(source, source + steps) for source in range(f...  8.41 us
    select_n x2, other arithmetic, local(): window = jnp.take(neighbourhood, row_index, axis=0)  8.33 us
    dot_general x1, matrix products, local(): jnp.einsum('pqij,pjk->pqik', blocks, masked, preferred_element_type=jnp.f...  8.28 us
    unnamed x6, local copies, waits for them, and re-layouts  7.37 us
  transfers between devices with their start and end apart: 7, of which 5 were waited for; matrix products, arithmetic and copies ran while one was open for 7% of the time, Pallas kernels for 0%

profile of v1, /device:TPU:0, one launch (start us, length us, event | category | flops | bytes accessed | tf_op | source)
XLA Modules:
  0.0 156.3 jit_solution(1828819601898236460)
XLA Ops:
  0.0 3.0 %collective-permute-start = (bf16[1,8,5,32,128]{4,3,2,1,0:T(8,128)(2,1)}, bf16[1,8,5,32,128]{4,3,2,1,0:T(8,128)(2,1)S(1)}, u32[]{:S(2)}, u32[]{:S(2)}) collective-permute-start(bf16[1,8,5,32,128]{4,3,2,1,0:T(8,128)(2,1)} %param.7), channel_id=1, source_target_pairs={{0,1},{1,2},{2,3},{3,0},{4,5},{5,6},{6,7},{7,4},{8,9},{9,10},{10,1... | collective-permute-start | bytes 983048 | tf_op jit(solution)/shard_map/ppermute | solution.py:24
  3.0 2.0 %collective-permute-start.1 = (bf16[1,8,5,32,128]{4,3,2,1,0:T(8,128)(2,1)}, bf16[1,8,5,32,128]{4,3,2,1,0:T(8,128)(2,1)S(1)}, u32[]{:S(2)}, u32[]{:S(2)}) collective-permute-start(bf16[1,8,5,32,128]{4,3,2,1,0:T(8,128)(2,1)} %param.7), channel_id=1, source_target_pairs={{0,3},{1,0},{2,1},{3,2},{4,7},{5,4},{6,5},{7,6},{8,11},{9,8},{10,9... | collective-permute-start | bytes 983048 | tf_op jit(solution)/shard_map/ppermute | solution.py:29
  5.1 8.8 %collective-permute-done = bf16[1,8,5,32,128]{4,3,2,1,0:T(8,128)(2,1)S(1)} collective-permute-done((bf16[1,8,5,32,128]{4,3,2,1,0:T(8,128)(2,1)}, bf16[1,8,5,32,128]{4,3,2,1,0:T(8,128)(2,1)S(1)}, u32[]{:S(2)}, u32[]{:S(2)}) %collective-permute-start) | collective-permute-done | bytes 327712 | tf_op jit(solution)/shard_map/ppermute | solution.py:24
  13.8 0.3 broadcast_in_dim.28
  14.1 1.0 constant_dynamic-update-slice_fusion.8
  15.2 4.4 %collective-permute-done.1 = bf16[1,8,5,32,128]{4,3,2,1,0:T(8,128)(2,1)S(1)} collective-permute-done((bf16[1,8,5,32,128]{4,3,2,1,0:T(8,128)(2,1)}, bf16[1,8,5,32,128]{4,3,2,1,0:T(8,128)(2,1)S(1)}, u32[]{:S(2)}, u32[]{:S(2)}) %collective-permute-start.1) | collective-permute-done | bytes 327712 | tf_op jit(solution)/shard_map/ppermute | solution.py:29
  19.7 7.4 %collective-permute-done.2 = bf16[1,8,5,32,128]{4,3,2,1,0:T(8,128)(2,1)S(1)} collective-permute-done((bf16[1,8,5,32,128]{4,3,2,1,0:T(8,128)(2,1)S(1)}, bf16[1,8,5,32,128]{4,3,2,1,0:T(8,128)(2,1)S(1)}, u32[]{:S(2)}, u32[]{:S(2)}) %collective-permute-start.2) | collective-permute-done | bytes 327712 | tf_op jit(solution)/shard_map/ppermute | solution.py:24
  27.1 3.5 %collective-permute-start.3 = (bf16[1,8,5,128,128]{4,3,2,1,0:T(8,128)(2,1)S(1)}, bf16[1,8,5,128,128]{4,3,2,1,0:T(8,128)(2,1)S(1)}, u32[]{:S(2)}, u32[]{:S(2)}) collective-permute-start(bf16[1,8,5,128,128]{4,3,2,1,0:T(8,128)(2,1)S(1)} %constant_dynamic-update-slice_fusion.5), channel_id=1, source_target_pairs={{0,8},{4,12},{8,16},{12,20},{16,24},{20,28},{1,9},{5,13},{9,17},{1... | collective-permute-start | bytes 3932168 | tf_op jit(solution)/shard_map/ppermute | solution.py:39
  30.6 2.4 %collective-permute-start.4 = (bf16[1,8,5,128,128]{4,3,2,1,0:T(8,128)(2,1)S(1)}, bf16[1,8,5,128,128]{4,3,2,1,0:T(8,128)(2,1)}, u32[]{:S(2)}, u32[]{:S(2)}) collective-permute-start(bf16[1,8,5,128,128]{4,3,2,1,0:T(8,128)(2,1)S(1)} %constant_dynamic-update-slice_fusion.5), channel_id=1, source_target_pairs={{0,4},{4,8},{8,12},{12,16},{16,20},{20,24},{24,28},{1,5},{5,9},{9,... | collective-permute-start | bytes 3932168 | tf_op jit(solution)/shard_map/ppermute | solution.py:39
  33.0 0.7 subtract_add_fusion
  33.6 1.3 collective-permute-start.5
  34.9 0.1 compare_select_fusion
  35.0 0.1 reshape.71
  35.1 1.3 collective-permute-start.6
  36.4 0.1 fusion.17
  36.4 0.1 copy.7
  36.5 0.7 broadcast_compare_fusion
  37.2 0.1 copy.6
  37.3 0.1 broadcast_bitcast_fusion
  37.4 22.3 %collective-permute-done.3 = bf16[1,8,5,128,128]{4,3,2,1,0:T(8,128)(2,1)S(1)} collective-permute-done((bf16[1,8,5,128,128]{4,3,2,1,0:T(8,128)(2,1)S(1)}, bf16[1,8,5,128,128]{4,3,2,1,0:T(8,128)(2,1)S(1)}, u32[]{:S(2)}, u32[]{:S(2)}) %collective-permute-start.3) | collective-permute-done | bytes 1310752 | tf_op jit(solution)/shard_map/ppermute | solution.py:39
  59.7 1.1 constant_dynamic-update-slice_fusion.4
  60.9 2.5 %constant_dynamic-update-slice_fusion.3 = bf16[5,8,5,128,128]{4,3,2,1,0:T(8,128)(2,1)} fusion(bf16[5,8,5,128,128]{4,3,2,1,0:T(8,128)(2,1)} %constant_dynamic-update-slice_fusion.4, bf16[1,8,5,128,128]{4,3,2,1,0:T(8,128)(2,1)} %collective-permute-done.4), kind=kLoop, calls=%fused_computation.24 | loop fusion | bytes 2621440
  63.4 1.1 constant_dynamic-update-slice_fusion.2
  64.6 2.5 %constant_dynamic-update-slice_fusion.1 = bf16[5,8,5,128,128]{4,3,2,1,0:T(8,128)(2,1)} fusion(bf16[5,8,5,128,128]{4,3,2,1,0:T(8,128)(2,1)} %constant_dynamic-update-slice_fusion.2, bf16[1,8,5,128,128]{4,3,2,1,0:T(8,128)(2,1)} %collective-permute-done.5), kind=kLoop, calls=%fused_computation.22 | loop fusion | bytes 2621440
  67.1 47.6 %collective-permute-done.6 = bf16[1,8,5,128,128]{4,3,2,1,0:T(8,128)(2,1)} collective-permute-done((bf16[1,8,5,128,128]{4,3,2,1,0:T(8,128)(2,1)S(1)}, bf16[1,8,5,128,128]{4,3,2,1,0:T(8,128)(2,1)}, u32[]{:S(2)}, u32[]{:S(2)}) %collective-permute-start.6) | collective-permute-done | bytes 1310752 | tf_op jit(solution)/shard_map/ppermute | solution.py:39
  114.7 2.6 %constant_dynamic-update-slice_fusion = bf16[5,8,5,128,128]{4,3,2,1,0:T(8,128)(2,1)} fusion(bf16[5,8,5,128,128]{4,3,2,1,0:T(8,128)(2,1)} %constant_dynamic-update-slice_fusion.1, bf16[1,8,5,128,128]{4,3,2,1,0:T(8,128)(2,1)} %collective-permute-done.6), kind=kLoop, calls=%fused_computation.21 | loop fusion | bytes 2621440 | tf_op jit(solution)/shard_map/concatenate | solution.py:61
  117.2 10.0 %gather_fusion = bf16[12,8,5,128,128]{4,3,2,1,0:T(8,128)(2,1)} fusion(bf16[5,8,5,128,128]{4,3,2,1,0:T(8,128)(2,1)} %constant_dynamic-update-slice_fusion, s32[1024]{0:T(1024)S(1)} %pad_clamp_fusion), kind=kCustom, calls=%fused_computation | custom fusion | bytes 31457328 | tf_op jit(solution)/shard_map/jit(_take)/gather | solution.py:65
  127.3 8.3 %copy_select_fusion = bf16[4,3,8,5,128,128]{5,4,2,0,3,1:T(8,128)(2,1)S(1)} fusion(bf16[4,3,8,5,128,128]{5,4,3,2,1,0:T(8,128)(2,1)} %bitcast.39, pred[4,3]{0,1:T(4,128)(4,1)S(1)} %copy.7), kind=kLoop, calls=%fused_computation.1 | loop fusion | flops 7864320 | bytes 31457292 | tf_op jit(solution)/shard_map/jit(_take)/select_n | solution.py:65
  135.5 0.0 copy-start
  135.5 3.7 %slice_bitcast_fusion.8 = (bf16[4,8,128,128]{3,2,1,0:T(8,128)(2,1)S(1)}, bf16[4,8,128,128]{3,2,1,0:T(8,128)(2,1)S(1)}, bf16[4,8,128,128]{3,2,1,0:T(8,128)(2,1)S(...) fusion(bf16[4,3,8,5,128,128]{5,4,2,0,3,1:T(8,128)(2,1)S(1)} %co, ...), kind=kLoop, calls=%fused_computation.19 | loop fusion | bytes 18874368 | tf_op jit(solution)/shard_map/squeeze | solution.py:46
  139.3 8.3 %fusion.29 = bf16[4,8,384,384]{3,2,1,0:T(8,128)(2,1)} fusion(bf16[4,8,128,128]{3,2,1,0:T(8,128)(2,1)S(1)} %get-tuple-element.6, bf16[4,8,128,128]{3,2,1,0:T(8,128)(2,1)S(1)} %get-tuple-element.7, bf16[4,8,128,128]{3,2,1,0:T(8,128)(2,1)S(1)} %get-tuple-element.8, bf16[4,8,128,128]{3,2,1,0:T(8,128)(2,1)S(1)} %get-tuple-element.9, ...), kind=kOutput, calls=%fused_computation.4.clone.clone.clone.2 | convolution fusion | flops 3714711552 | bytes 20055552 | tf_op jit(solution)/shard_map/pqij,pjk->pqik/dot_general | solution.py:70
  147.6 8.7 %and_select_fusion = f32[4,384,384]{2,1,0:T(8,128)} fusion(bf16[4,8,128,128]{3,2,1,0:T(8,128)(2,1)S(1)} %get-tuple-element.6, bf16[4,8,128,128]{3,2,1,0:T(8,128)(2,1)S(1)} %get-tuple-element.7, bf16[4,8,128,128]{3,2,1,0:T(8,128)(2,1)S(1)} %get-tuple-element.8, bf16[4,8,128,128]{3,2,1,0:T(8,128)(2,1)S(1)} %get-tuple-element.9, ...), kind=kOutput, calls=%fused_computation.6 | convolution fusion | flops 3709992960 | bytes 21235200 | tf_op jit(solution)/shard_map/pqik,pqlk->pil/dot_general | solution.py:73
  (8 shorter events, 0.2 us)
Async XLA Ops:
  0.0 13.8 %collective-permute-start = (bf16[1,8,5,32,128]{4,3,2,1,0:T(8,128)(2,1)}, bf16[1,8,5,32,128]{4,3,2,1,0:T(8,128)(2,1)S(1)}, u32[]{:S(2)}, u32[]{:S(2)}) collective-permute-start(bf16[1,8,5,32,128]{4,3,2,1,0:T(8,128)(2,1)} %param.7), channel_id=1, source_target_pairs={{0,1},{1,2},{2,3},{3,0},{4,5},{5,6},{6,7},{7,4},{8,9},{9,10},{10,1... | collective-permute-start | bytes 983048 | tf_op jit(solution)/shard_map/ppermute | solution.py:24
  3.0 16.6 %collective-permute-start.1 = (bf16[1,8,5,32,128]{4,3,2,1,0:T(8,128)(2,1)}, bf16[1,8,5,32,128]{4,3,2,1,0:T(8,128)(2,1)S(1)}, u32[]{:S(2)}, u32[]{:S(2)}) collective-permute-start(bf16[1,8,5,32,128]{4,3,2,1,0:T(8,128)(2,1)} %param.7), channel_id=1, source_target_pairs={{0,3},{1,0},{2,1},{3,2},{4,7},{5,4},{6,5},{7,6},{8,11},{9,8},{10,9... | collective-permute-start | bytes 983048 | tf_op jit(solution)/shard_map/ppermute | solution.py:29
  13.8 13.2 %collective-permute-start.2 = (bf16[1,8,5,32,128]{4,3,2,1,0:T(8,128)(2,1)S(1)}, bf16[1,8,5,32,128]{4,3,2,1,0:T(8,128)(2,1)S(1)}, u32[]{:S(2)}, u32[]{:S(2)}) collective-permute-start(bf16[1,8,5,32,128]{4,3,2,1,0:T(8,128)(2,1)S(1)} %collective-permute-done), channel_id=1, source_target_pairs={{0,1},{1,2},{2,3},{3,0},{4,5},{5,6},{6,7},{7,4},{8,9},{9,10},{10,1... | collective-permute-start | bytes 983048 | tf_op jit(solution)/shard_map/ppermute | solution.py:24
  27.1 32.6 %collective-permute-start.3 = (bf16[1,8,5,128,128]{4,3,2,1,0:T(8,128)(2,1)S(1)}, bf16[1,8,5,128,128]{4,3,2,1,0:T(8,128)(2,1)S(1)}, u32[]{:S(2)}, u32[]{:S(2)}) collective-permute-start(bf16[1,8,5,128,128]{4,3,2,1,0:T(8,128)(2,1)S(1)} %constant_dynamic-update-slice_fusion.5), channel_id=1, source_target_pairs={{0,8},{4,12},{8,16},{12,20},{16,24},{20,28},{1,9},{5,13},{9,17},{1... | collective-permute-start | bytes 3932168 | tf_op jit(solution)/shard_map/ppermute | solution.py:39
  30.6 30.3 %collective-permute-start.4 = (bf16[1,8,5,128,128]{4,3,2,1,0:T(8,128)(2,1)S(1)}, bf16[1,8,5,128,128]{4,3,2,1,0:T(8,128)(2,1)}, u32[]{:S(2)}, u32[]{:S(2)}) collective-permute-start(bf16[1,8,5,128,128]{4,3,2,1,0:T(8,128)(2,1)S(1)} %constant_dynamic-update-slice_fusion.5), channel_id=1, source_target_pairs={{0,4},{4,8},{8,12},{12,16},{16,20},{20,24},{24,28},{1,5},{5,9},{9,... | collective-permute-start | bytes 3932168 | tf_op jit(solution)/shard_map/ppermute | solution.py:39
  33.6 30.9 %collective-permute-start.5 = (bf16[1,8,5,128,128]{4,3,2,1,0:T(8,128)(2,1)S(1)}, bf16[1,8,5,128,128]{4,3,2,1,0:T(8,128)(2,1)}, u32[]{:S(2)}, u32[]{:S(2)}) collective-permute-start(bf16[1,8,5,128,128]{4,3,2,1,0:T(8,128)(2,1)S(1)} %constant_dynamic-update-slice_fusion.5), channel_id=1, source_target_pairs={{4,0},{8,4},{12,8},{16,12},{20,16},{24,20},{28,24},{5,1},{9,5},{13... | collective-permute-start | bytes 3932168 | tf_op jit(solution)/shard_map/ppermute | solution.py:39
  35.1 79.6 %collective-permute-start.6 = (bf16[1,8,5,128,128]{4,3,2,1,0:T(8,128)(2,1)S(1)}, bf16[1,8,5,128,128]{4,3,2,1,0:T(8,128)(2,1)}, u32[]{:S(2)}, u32[]{:S(2)}) collective-permute-start(bf16[1,8,5,128,128]{4,3,2,1,0:T(8,128)(2,1)S(1)} %constant_dynamic-update-slice_fusion.5), channel_id=1, source_target_pairs={{8,0},{12,4},{16,8},{20,12},{24,16},{28,20},{9,1},{13,5},{17,9},{2... | collective-permute-start | bytes 3932168 | tf_op jit(solution)/shard_map/ppermute | solution.py:39
  135.5 3.8 %copy-start = (bf16[4,384,384]{2,1,0:T(8,128)(2,1)S(1)}, bf16[4,384,384]{2,1,0:T(8,128)(2,1)}, u32[]{:S(2)}) copy-start(bf16[4,384,384]{2,1,0:T(8,128)(2,1)} %param.4) | copy-start | bytes 3538948
